TPU v7x, 32 devices: a whole 2x2x4 slice. The times are simulated.
32 devices in a mesh: grp: 2 (over x), seq: 16 (over z, y, core).
Axes of the slice: x: 2, y: 2, z: 4, core: 2. Of those that a mesh axis runs over, the one named last changes fastest.
Arguments:
- queries: bfloat16 [16384, 2048], P(('grp', 'seq')), parts along dimension 0, may hold values from -16 to 16
- key_rows: bfloat16 [16384, 2048], P(('grp', 'seq')), parts along dimension 0, may hold values from -4 to 4
- value_rows: bfloat16 [16384, 2048], P(('grp', 'seq')), parts along dimension 0, may hold values from -6 to 6
- box_bins: int32 [2, 16384], P(None, ('grp', 'seq')), parts along dimension 1, may hold values from 0 to 255
- slopes: float32 [16], replicated, may hold values from 0.05 to 3
- near_lists: int32 [128, 5], P('grp'), parts along dimension 0, may hold values from -1 to 59, as said below
Outputs:
- attended: bfloat16 [16384, 2048], P(('grp', 'seq')), parts along dimension 0
There are 2 independent parts, one for each index of `grp`. A program takes and returns all parts, laid end to end along the dimension named above; an argument that names none is the same for every part. Nothing has to cross between parts.
Inputs may be any that keep to these rules, and one draw needn't show every extreme that they name: `near_lists`: block ids lie on one of the 6 devices before the query block's device, the device of block c being c // 4; the ids listed for one query block differ from one another; the lists of one device's 4 query blocks together name exactly 2 distinct blocks of each of those preceding devices that exist, and -1 stands for the blocks of devices before the first.
All inputs are finite; a program needn't handle non-finite values.
Results may differ from a plain program's by a relative error of at most 0.0038.
Values may be sent and summed in bfloat16 or wider, within the bound.
A program may use at most 128 MiB of HBM per device.

v0:
```python
import math
import jax
import jax.numpy as jnp
from jax import lax
from jax.sharding import PartitionSpec as P

BLOCK = 128
REACH = 6


def shifted(shard, axis, by):
    peers = lax.axis_size(axis)
    pairs = [(i, i + by) for i in range(peers) if 0 <= i + by < peers]
    return lax.ppermute(shard, axis, pairs)


def attend(query_block, all_keys, all_values, query_bins, key_bins, present, slopes):
    row_count, features = query_block.shape
    head_count = slopes.shape[0]
    head_dim = features // head_count
    key_count = all_keys.shape[0]
    products = jnp.einsum(
        "qhd,khd->hqk",
        query_block.reshape(row_count, head_count, head_dim),
        all_keys.reshape(key_count, head_count, head_dim),
        preferred_element_type=jnp.float32,
    )
    query_spot = query_bins.astype(jnp.float32)
    key_spot = key_bins.astype(jnp.float32)
    spread = jnp.abs(query_spot[0][:, None] - key_spot[0][None, :]) + jnp.abs(
        query_spot[1][:, None] - key_spot[1][None, :]
    )
    scores = (
        products * (1.0 / math.sqrt(head_dim)) - slopes[:, None, None] * (spread * 0.015625)[None]
    )
    row_ids = jnp.arange(row_count, dtype=jnp.int32)[:, None]
    col_ids = jnp.arange(key_count, dtype=jnp.int32)[None, :]
    listed = jnp.concatenate([jnp.ones((row_count,), bool), jnp.repeat(present, row_count)])[
        None, :
    ]
    allowed = jnp.where(col_ids < row_count, col_ids <= row_ids, listed)
    masked = jnp.where(allowed[None], scores, -jnp.inf)
    largest = jnp.max(masked, axis=2, keepdims=True)
    exponent = jnp.exp(masked - largest)
    totals = jnp.sum(exponent, axis=2)
    weights = exponent.astype(jnp.bfloat16)
    mixture = jnp.einsum(
        "hqk,khd->qhd",
        weights,
        all_values.reshape(key_count, head_count, head_dim),
        preferred_element_type=jnp.float32,
    )
    return (
        (mixture / jnp.transpose(totals)[:, :, None])
        .reshape(row_count, features)
        .astype(jnp.bfloat16)
    )


def body(queries, key_rows, value_rows, box_bins, slopes, near_lists):
    token_count, features = queries.shape
    blocks = token_count // BLOCK
    device = lax.axis_index("seq")
    query_blocks = queries.reshape(blocks, BLOCK, features)
    key_blocks = key_rows.reshape(blocks, BLOCK, features)
    value_blocks = value_rows.reshape(blocks, BLOCK, features)
    own_bins = jnp.transpose(box_bins.reshape(2, blocks, BLOCK), (1, 0, 2))
    every_bins = lax.all_gather(box_bins, "seq", axis=1, tiled=True)
    all_bins = jnp.transpose(every_bins.reshape(2, -1, BLOCK), (1, 0, 2))
    own_lists = lax.dynamic_slice_in_dim(near_lists, device * blocks, blocks, 0)
    present = own_lists >= 0
    clamped = jnp.maximum(own_lists, 0)
    distance = device - clamped // blocks
    block_slot = clamped % blocks
    arrivals = [shifted((key_rows, value_rows), "seq", offset) for offset in range(1, REACH + 1)]
    window_keys = jnp.stack([arrived[0] for arrived in arrivals]).reshape(
        REACH * blocks, BLOCK, features
    )
    window_values = jnp.stack([arrived[1] for arrived in arrivals]).reshape(
        REACH * blocks, BLOCK, features
    )
    slot_index = (distance - 1) * blocks + block_slot
    slot_index = jnp.where(present, slot_index, 0)

    def one_block(inputs):
        query_block, own_keys, own_values, query_bins, slots, listed_ids, listed_present = inputs
        all_keys = jnp.concatenate(
            [own_keys[None], jnp.take(window_keys, slots, axis=0)], 0
        ).reshape(-1, features)
        all_values = jnp.concatenate(
            [own_values[None], jnp.take(window_values, slots, axis=0)], 0
        ).reshape(-1, features)
        key_bins = jnp.concatenate([query_bins[None], jnp.take(all_bins, listed_ids, axis=0)], 0)
        key_bins = jnp.transpose(key_bins, (1, 0, 2)).reshape(2, -1)
        return attend(
            query_block, all_keys, all_values, query_bins, key_bins, listed_present, slopes
        )

    results = lax.map(
        one_block, (query_blocks, key_blocks, value_blocks, own_bins, slot_index, clamped, present)
    )
    return results.reshape(token_count, features)


def solution(mesh):
    placed = (
        P(("grp", "seq"), None),
        P(("grp", "seq"), None),
        P(("grp", "seq"), None),
        P(None, ("grp", "seq")),
        P(),
        P("grp", None),
    )
    return jax.shard_map(
        body, mesh=mesh, in_specs=placed, out_specs=P(("grp", "seq"), None), check_vma=False
    )
```

profile of v0, /device:TPU:25, one launch (start us, length us, event | category | flops | bytes accessed | tf_op | source)
XLA Modules:
  0.0 809.9 jit_solution(5328308519130120279)
XLA Ops:
  0.0 3.8 collective-permute-start
  3.8 1.9 collective-permute-start.6
  5.8 1.9 collective-permute-start.1
  7.7 1.3 collective-permute-start.2
  9.0 1.3 collective-permute-start.3
  10.5 183.5 %all_gather.3 = s32[2,8192]{1,0:T(2,128)S(1)} all-gather(s32[2,512]{1,0:T(2,128)} %param.13), channel_id=1, replica_groups=mesh['grp'=2,'seq'=16] {'seq'}, dimensions={1}, use_global_device_ids=true | all-gather | bytes 69632 | tf_op jit(solution)/shard_map/all_gather | solution.py:68
  194.5 1.3 collective-permute-start.4
  195.8 1.7 bitcast_dynamic-update-slice_fusion.11
  197.6 1.4 collective-permute-start.5
  199.0 1.7 bitcast_dynamic-update-slice_fusion.5
  200.7 1.9 collective-permute-start.7
  202.7 1.7 bitcast_dynamic-update-slice_fusion.10
  204.4 1.3 collective-permute-start.8
  205.7 1.7 bitcast_dynamic-update-slice_fusion.9
  207.5 1.3 collective-permute-start.9
  208.9 35.9 %collective-permute-done.4 = bf16[512,2048]{1,0:T(8,128)(2,1)S(1)} collective-permute-done((bf16[512,2048]{1,0:T(8,128)(2,1)}, bf16[512,2048]{1,0:T(8,128)(2,1)S(1)}, u32[]{:S(2)}, u32[]{:S(2)}) %collective-permute-start.4) | collective-permute-done | bytes 2097184 | tf_op jit(solution)/shard_map/ppermute | solution.py:14
  244.8 1.3 collective-permute-start.10
  246.4 111.8 %collective-permute-done.5 = bf16[512,2048]{1,0:T(8,128)(2,1)S(1)} collective-permute-done((bf16[512,2048]{1,0:T(8,128)(2,1)}, bf16[512,2048]{1,0:T(8,128)(2,1)S(1)}, u32[]{:S(2)}, u32[]{:S(2)}) %collective-permute-start.5) | collective-permute-done | bytes 2097184 | tf_op jit(solution)/shard_map/ppermute | solution.py:14
  358.2 1.5 collective-permute-start.11
  360.1 35.5 %collective-permute-done.8 = bf16[512,2048]{1,0:T(8,128)(2,1)S(1)} collective-permute-done((bf16[512,2048]{1,0:T(8,128)(2,1)S(1)}, bf16[512,2048]{1,0:T(8,128)(2,1)S(1)}, u32[]{:S(2)}, u32[]{:S(2)}) %collective-permute-start.8) | collective-permute-done | bytes 2097184 | tf_op jit(solution)/shard_map/ppermute | solution.py:14
  396.4 252.1 %collective-permute-done.11 = bf16[512,2048]{1,0:T(8,128)(2,1)S(1)} collective-permute-done((bf16[512,2048]{1,0:T(8,128)(2,1)S(1)}, bf16[512,2048]{1,0:T(8,128)(2,1)S(1)}, u32[]{:S(2)}, u32[]{:S(2)}) %collective-permute-start.11) | collective-permute-done | bytes 2097184 | tf_op jit(solution)/shard_map/ppermute | solution.py:14
  648.8 4.5 copy-done.2
  653.2 155.9 %while.10 = (s32[]{:T(128)}, bf16[4,128,2048]{2,1,0:T(8,128)(2,1)}, bf16[4,128,2048]{2,1,0:T(8,128)(2,1)}, s32[4,5]{1,0:T(4,128)S(1)}, bf16[24,128,2048]{2,1,0:T...) while((s32[]{:T(128)}, bf16[4,128,2048]{2,1,0:T(8,128)(2,1)}, ...), condition=%wide.region_3.5_spmd, body=%wide.region_0.4_spmd.sunk | while | flops 839126336 | bytes 81245688 | solution.py:99
  654.8 7.1 gather_fusion.2
  661.9 7.0 gather_fusion.1
  668.9 3.1 broadcast_select_fusion.6
  672.0 1.3 constant_dynamic-slice_fusion.11
  673.6 2.7 copy.49
  676.3 1.0 copy.48
  677.4 5.3 fusion.55
  682.8 2.1 fusion.56
  684.9 1.1 constant_dynamic-slice_fusion.12
  686.3 1.0 copy.50
  687.3 3.9 divide_convert_fusion.2
  693.8 7.1 gather_fusion.2
  700.9 7.0 gather_fusion.1
  707.9 3.1 broadcast_select_fusion.6
  711.0 1.3 constant_dynamic-slice_fusion.11
  712.5 2.7 copy.49
  715.3 1.0 copy.48
  716.4 5.3 fusion.55
  721.7 2.1 fusion.56
  723.9 1.1 constant_dynamic-slice_fusion.12
  725.2 1.0 copy.50
  726.3 3.9 divide_convert_fusion.2
  732.8 7.1 gather_fusion.2
  739.9 7.0 gather_fusion.1
  746.9 3.1 broadcast_select_fusion.6
  749.9 1.3 constant_dynamic-slice_fusion.11
  751.5 2.7 copy.49
  754.2 1.0 copy.48
  755.4 5.3 fusion.55
  760.7 2.1 fusion.56
  762.8 1.1 constant_dynamic-slice_fusion.12
  765.2 3.9 divide_convert_fusion.2
  771.8 7.1 gather_fusion.2
  778.8 7.0 gather_fusion.1
  785.9 3.1 broadcast_select_fusion.6
  788.9 1.3 constant_dynamic-slice_fusion.11
  790.5 2.7 copy.49
  794.4 5.3 fusion.55
  799.7 2.1 fusion.56
  801.8 1.1 constant_dynamic-slice_fusion.12
  804.2 3.9 divide_convert_fusion.2
  (138 shorter events, 19.5 us)
Async XLA Ops:
  0.0 10.3 %copy-start = (s32[64,5]{0,1:T(8,128)S(1)}, s32[64,5]{0,1:T(8,128)}, u32[]{:S(2)}) copy-start(s32[64,5]{0,1:T(8,128)} %param.15) | copy-start | bytes 3844
  0.0 194.5 %collective-permute-start = (bf16[512,2048]{1,0:T(8,128)(2,1)}, bf16[512,2048]{1,0:T(8,128)(2,1)}, u32[]{:S(2)}, u32[]{:S(2)}) collective-permute-start(bf16[512,2048]{1,0:T(8,128)(2,1)} %param.12), channel_id=1, source_target_pairs={{0,1},{1,2},{2,3},{3,4},{4,5},{5,6},{6,7},{7,8},{8,9},{9,10},{10,1... | collective-permute-start | bytes 6291464 | tf_op jit(solution)/shard_map/ppermute | solution.py:14
  3.8 193.7 %collective-permute-start.6 = (bf16[512,2048]{1,0:T(8,128)(2,1)}, bf16[512,2048]{1,0:T(8,128)(2,1)}, u32[]{:S(2)}, u32[]{:S(2)}) collective-permute-start(bf16[512,2048]{1,0:T(8,128)(2,1)} %param.11), channel_id=1, source_target_pairs={{0,1},{1,2},{2,3},{3,4},{4,5},{5,6},{6,7},{7,8},{8,9},{9,10},{10,1... | collective-permute-start | bytes 6291464 | tf_op jit(solution)/shard_map/ppermute | solution.py:14
  5.8 195.0 %collective-permute-start.1 = (bf16[512,2048]{1,0:T(8,128)(2,1)}, bf16[512,2048]{1,0:T(8,128)(2,1)}, u32[]{:S(2)}, u32[]{:S(2)}) collective-permute-start(bf16[512,2048]{1,0:T(8,128)(2,1)} %param.12), channel_id=1, source_target_pairs={{0,2},{1,3},{2,4},{3,5},{4,6},{5,7},{6,8},{7,9},{8,10},{9,11},{10,... | collective-permute-start | bytes 6291464 | tf_op jit(solution)/shard_map/ppermute | solution.py:14
  7.7 196.7 %collective-permute-start.2 = (bf16[512,2048]{1,0:T(8,128)(2,1)}, bf16[512,2048]{1,0:T(8,128)(2,1)}, u32[]{:S(2)}, u32[]{:S(2)}) collective-permute-start(bf16[512,2048]{1,0:T(8,128)(2,1)} %param.12), channel_id=1, source_target_pairs={{0,3},{1,4},{2,5},{3,6},{4,7},{5,8},{6,9},{7,10},{8,11},{9,12},{10... | collective-permute-start | bytes 6291464 | tf_op jit(solution)/shard_map/ppermute | solution.py:14
  9.0 198.5 %collective-permute-start.3 = (bf16[512,2048]{1,0:T(8,128)(2,1)}, bf16[512,2048]{1,0:T(8,128)(2,1)S(1)}, u32[]{:S(2)}, u32[]{:S(2)}) collective-permute-start(bf16[512,2048]{1,0:T(8,128)(2,1)} %param.12), channel_id=1, source_target_pairs={{0,4},{1,5},{2,6},{3,7},{4,8},{5,9},{6,10},{7,11},{8,12},{9,13},{1... | collective-permute-start | bytes 6291464 | tf_op jit(solution)/shard_map/ppermute | solution.py:14
  194.5 50.3 %collective-permute-start.4 = (bf16[512,2048]{1,0:T(8,128)(2,1)}, bf16[512,2048]{1,0:T(8,128)(2,1)S(1)}, u32[]{:S(2)}, u32[]{:S(2)}) collective-permute-start(bf16[512,2048]{1,0:T(8,128)(2,1)} %param.12), channel_id=1, source_target_pairs={{0,5},{1,6},{2,7},{3,8},{4,9},{5,10},{6,11},{7,12},{8,13},{9,14},{... | collective-permute-start | bytes 6291464 | tf_op jit(solution)/shard_map/ppermute | solution.py:14
  197.5 3.2 copy-start.4
  197.6 160.6 %collective-permute-start.5 = (bf16[512,2048]{1,0:T(8,128)(2,1)}, bf16[512,2048]{1,0:T(8,128)(2,1)S(1)}, u32[]{:S(2)}, u32[]{:S(2)}) collective-permute-start(bf16[512,2048]{1,0:T(8,128)(2,1)} %param.12), channel_id=1, source_target_pairs={{0,6},{1,7},{2,8},{3,9},{4,10},{5,11},{6,12},{7,13},{8,14},{9,15},... | collective-permute-start | bytes 6291464 | tf_op jit(solution)/shard_map/ppermute | solution.py:14
  200.7 159.1 %collective-permute-start.7 = (bf16[512,2048]{1,0:T(8,128)(2,1)S(1)}, bf16[512,2048]{1,0:T(8,128)(2,1)S(1)}, u32[]{:S(2)}, u32[]{:S(2)}) collective-permute-start(bf16[512,2048]{1,0:T(8,128)(2,1)S(1)} %copy-done.4), channel_id=1, source_target_pairs={{0,2},{1,3},{2,4},{3,5},{4,6},{5,7},{6,8},{7,9},{8,10},{9,11},{10,... | collective-permute-start | bytes 6291464 | tf_op jit(solution)/shard_map/ppermute | solution.py:14
  204.4 191.2 %collective-permute-start.8 = (bf16[512,2048]{1,0:T(8,128)(2,1)S(1)}, bf16[512,2048]{1,0:T(8,128)(2,1)S(1)}, u32[]{:S(2)}, u32[]{:S(2)}) collective-permute-start(bf16[512,2048]{1,0:T(8,128)(2,1)S(1)} %copy-done.4), channel_id=1, source_target_pairs={{0,3},{1,4},{2,5},{3,6},{4,7},{5,8},{6,9},{7,10},{8,11},{9,12},{10... | collective-permute-start | bytes 6291464 | tf_op jit(solution)/shard_map/ppermute | solution.py:14
  207.5 188.4 %collective-permute-start.9 = (bf16[512,2048]{1,0:T(8,128)(2,1)S(1)}, bf16[512,2048]{1,0:T(8,128)(2,1)S(1)}, u32[]{:S(2)}, u32[]{:S(2)}) collective-permute-start(bf16[512,2048]{1,0:T(8,128)(2,1)S(1)} %copy-done.4), channel_id=1, source_target_pairs={{0,4},{1,5},{2,6},{3,7},{4,8},{5,9},{6,10},{7,11},{8,12},{9,13},{1... | collective-permute-start | bytes 6291464 | tf_op jit(solution)/shard_map/ppermute | solution.py:14
  244.8 151.3 %collective-permute-start.10 = (bf16[512,2048]{1,0:T(8,128)(2,1)S(1)}, bf16[512,2048]{1,0:T(8,128)(2,1)S(1)}, u32[]{:S(2)}, u32[]{:S(2)}) collective-permute-start(bf16[512,2048]{1,0:T(8,128)(2,1)S(1)} %copy-done.4), channel_id=1, source_target_pairs={{0,5},{1,6},{2,7},{3,8},{4,9},{5,10},{6,11},{7,12},{8,13},{9,14},{... | collective-permute-start | bytes 6291464 | tf_op jit(solution)/shard_map/ppermute | solution.py:14
  358.2 290.3 %collective-permute-start.11 = (bf16[512,2048]{1,0:T(8,128)(2,1)S(1)}, bf16[512,2048]{1,0:T(8,128)(2,1)S(1)}, u32[]{:S(2)}, u32[]{:S(2)}) collective-permute-start(bf16[512,2048]{1,0:T(8,128)(2,1)S(1)} %copy-done.4), channel_id=1, source_target_pairs={{0,6},{1,7},{2,8},{3,9},{4,10},{5,11},{6,12},{7,13},{8,14},{9,15},... | collective-permute-start | bytes 6291464 | tf_op jit(solution)/shard_map/ppermute | solution.py:14
  359.9 288.9 %copy-start.3 = (bf16[6,512,2048]{2,1,0:T(8,128)(2,1)}, bf16[6,512,2048]{2,1,0:T(8,128)(2,1)S(1)}, u32[]{:S(2)}) copy-start(bf16[6,512,2048]{2,1,0:T(8,128)(2,1)S(1)} %bitcast_dynamic-update-slice_fusion.6) | copy-start | bytes 37748740
  396.4 256.9 %copy-start.7 = (f32[16]{0:T(128)S(1)}, f32[16]{0:T(128)}, u32[]{:S(2)}) copy-start(f32[16]{0:T(128)} %param.14) | copy-start | bytes 196
  648.7 4.5 copy-start.2
  653.2 15.7 %copy-start.5 = (s32[64,2,128]{2,1,0:T(2,128)}, s32[64,2,128]{2,1,0:T(2,128)S(1)}, u32[]{:S(2)}) copy-start(s32[64,2,128]{2,1,0:T(2,128)S(1)} %get-tuple-element.282) | copy-start | bytes 196612 | tf_op jit(solution)/shard_map/while
  673.5 3.8 copy-start.8
  687.3 5.0 copy-start.6
  692.2 15.7 %copy-start.5 = (s32[64,2,128]{2,1,0:T(2,128)}, s32[64,2,128]{2,1,0:T(2,128)S(1)}, u32[]{:S(2)}) copy-start(s32[64,2,128]{2,1,0:T(2,128)S(1)} %get-tuple-element.282) | copy-start | bytes 196612 | tf_op jit(solution)/shard_map/while
  712.5 3.8 copy-start.8
  726.2 5.0 copy-start.6
  731.2 15.7 %copy-start.5 = (s32[64,2,128]{2,1,0:T(2,128)}, s32[64,2,128]{2,1,0:T(2,128)S(1)}, u32[]{:S(2)}) copy-start(s32[64,2,128]{2,1,0:T(2,128)S(1)} %get-tuple-element.282) | copy-start | bytes 196612 | tf_op jit(solution)/shard_map/while
  751.5 3.8 copy-start.8
  765.2 5.0 copy-start.6
  770.2 15.7 %copy-start.5 = (s32[64,2,128]{2,1,0:T(2,128)}, s32[64,2,128]{2,1,0:T(2,128)S(1)}, u32[]{:S(2)}) copy-start(s32[64,2,128]{2,1,0:T(2,128)S(1)} %get-tuple-element.282) | copy-start | bytes 196612 | tf_op jit(solution)/shard_map/while
  790.5 3.8 copy-start.8
  804.2 5.0 copy-start.6
  809.2 0.7 copy-start.1
where the time goes:
time: 811 us; the launch traced here: 810 us
  waiting for transfers between devices  435 us (54%)
  blocking collectives  184 us (23%)
  local copies, waits for them, and re-layouts  106 us (13%)
  matrix products  36.7 us (5%)
  other arithmetic  27.4 us (3%)
  starting transfers between devices  20.2 us (2%)
    ppermute x12, waiting for transfers between devices, shifted(): return lax.ppermute(shard, axis, pairs)  435 us
    all_gather x1, blocking collectives, body(): every_bins = lax.all_gather(box_bins, 'seq', axis=1, tiled=True)  184 us
    gather x4, local copies, waits for them, and re-layouts, one_block(): jnp.take(window_keys, slots, axis=0)  28.2 us
    gather x4, local copies, waits for them, and re-layouts, one_block(): jnp.take(window_values, slots, axis=0)  28 us
    dot_general x4, matrix products, attend(): jnp.einsum('qhd,khd->hqk', query_block.reshape(row_count, head_count, hea...  21.3 us
    ppermute x12, starting transfers between devices, shifted(): return lax.ppermute(shard, axis, pairs)  20.2 us
  transfers between devices with their start and end apart: 12, of which 4 were waited for; matrix products, arithmetic and copies ran while one was open for 1% of the time, Pallas kernels for 0%

commit v1 on v0

--- a/solution.py
+++ b/solution.py
@@ -65,7 +65,21 @@
     key_blocks = key_rows.reshape(blocks, BLOCK, features)
     value_blocks = value_rows.reshape(blocks, BLOCK, features)
     own_bins = jnp.transpose(box_bins.reshape(2, blocks, BLOCK), (1, 0, 2))
-    every_bins = lax.all_gather(box_bins, "seq", axis=1, tiled=True)
+    ways, here, step = (lax.axis_size("seq"), lax.axis_index("seq"), box_bins.shape[1])
+    shape = [n * ways if d == 1 else n for d, n in enumerate(box_bins.shape)]
+    full = lax.dynamic_update_slice_in_dim(
+        jnp.zeros(shape, box_bins.dtype), box_bins, here * step, axis=1
+    )
+    going_up = going_down = box_bins
+    for far in range(1, ways // 2 + 1):
+        going_up = lax.ppermute(going_up, "seq", [(d, (d + 1) % ways) for d in range(ways)])
+        full = lax.dynamic_update_slice_in_dim(full, going_up, (here - far) % ways * step, axis=1)
+        if 2 * far < ways:
+            going_down = lax.ppermute(going_down, "seq", [(d, (d - 1) % ways) for d in range(ways)])
+            full = lax.dynamic_update_slice_in_dim(
+                full, going_down, (here + far) % ways * step, axis=1
+            )
+    every_bins = full
     all_bins = jnp.transpose(every_bins.reshape(2, -1, BLOCK), (1, 0, 2))
     own_lists = lax.dynamic_slice_in_dim(near_lists, device * blocks, blocks, 0)
     present = own_lists >= 0

time: 811 us -> 836 us (1.031)
  blocking collectives: 184 us -> 0 us
  waiting for transfers between devices: 435 us -> 598 us
  starting transfers between devices: 20.2 us -> 68.4 us
    all_gather x1 -> x0, blocking collectives: 184 us -> none  [body(): every_bins = lax.all_gather(box_bins, 'seq', axis=1, tiled=True)]
    ppermute x0 -> x15, waiting for transfers between devices: none -> 119 us  [the longest x8 113 us: body(): lax.ppermute(going_up, 'seq', [(d, (d + 1) % ways) for d in range(ways)])]
    ppermute x0 -> x15, starting transfers between devices: none -> 43.8 us  [the longest x7 41.9 us: body(): lax.ppermute(going_down, 'seq', [(d, (d - 1) % ways) for d in range(ways)])]
    ppermute x12, waiting for transfers between devices: 435 us -> 478 us  [shifted(): return lax.ppermute(shard, axis, pairs)]
  transfers between devices with their start and end apart: 12 -> 27, of which waited for: 4 -> 18; matrix products, arithmetic and copies ran while one was open for 1% -> 1% of each run, Pallas kernels for 0% -> 0%
where the time goes in v1:
time: 836 us; the launch traced here: 835 us
  waiting for transfers between devices  598 us (72%)
  local copies, waits for them, and re-layouts  103 us (12%)
  starting transfers between devices  68.4 us (8%)
  matrix products  36.7 us (4%)
  other arithmetic  27.5 us (3%)
    ppermute x12, waiting for transfers between devices, shifted(): return lax.ppermute(shard, axis, pairs)  478 us
    ppermute x8, waiting for transfers between devices, body(): lax.ppermute(going_up, 'seq', [(d, (d + 1) % ways) for d in range(ways)])  113 us
    ppermute x7, starting transfers between devices, body(): lax.ppermute(going_down, 'seq', [(d, (d - 1) % ways) for d in range(ways)])  41.9 us
    gather x4, local copies, waits for them, and re-layouts, one_block(): jnp.take(window_keys, slots, axis=0)  28.1 us
    gather x4, local copies, waits for them, and re-layouts, one_block(): jnp.take(window_values, slots, axis=0)  28 us
    ppermute x12, starting transfers between devices, shifted(): return lax.ppermute(shard, axis, pairs)  24.5 us
    dot_general x4, matrix products, attend(): jnp.einsum('qhd,khd->hqk', query_block.reshape(row_count, head_count, hea...  21.3 us
  transfers between devices with their start and end apart: 27, of which 18 were waited for; matrix products, arithmetic and copies ran while one was open for 1% of the time, Pallas kernels for 0%

profile of v1, /device:TPU:25, one launch (start us, length us, event | category | flops | bytes accessed | tf_op | source)
XLA Modules:
  0.0 834.5 jit_solution(11497252117251716053)
XLA Ops:
  0.0 1.8 collective-permute-start.12
  1.8 3.6 collective-permute-start
  5.5 1.9 collective-permute-start.1
  7.4 1.3 collective-permute-start.2
  10.4 1.9 collective-permute-start.6
  12.4 106.2 %collective-permute-done.14 = s32[2,512]{1,0:T(2,128)S(1)} collective-permute-done((s32[2,512]{1,0:T(2,128)S(1)}, s32[2,512]{1,0:T(2,128)S(1)}, u32[]{:S(2)}, u32[]{:S(2)}) %collective-permute-start.14) | collective-permute-done | bytes 4128 | tf_op jit(solution)/shard_map/ppermute | solution.py:75
  118.7 25.6 %collective-permute-start.15 = (s32[2,512]{1,0:T(2,128)S(1)}, s32[2,512]{1,0:T(2,128)S(1)}, u32[]{:S(2)}, u32[]{:S(2)}) collective-permute-start(s32[2,512]{1,0:T(2,128)S(1)} %collective-permute-done.13), channel_id=1, source_target_pairs={{0,15},{1,0},{2,1},{3,2},{4,3},{5,4},{6,5},{7,6},{8,7},{9,8},{10,9... | collective-permute-start | bytes 12296 | tf_op jit(solution)/shard_map/ppermute | solution.py:78
  145.1 1.2 collective-permute-done.16
  146.2 3.3 collective-permute-start.17
  151.5 3.3 collective-permute-start.19
  156.7 3.3 collective-permute-start.21
  162.0 3.3 collective-permute-start.23
  166.1 1.2 collective-permute-done.24
  167.3 3.3 collective-permute-start.25
  170.6 2.1 collective-permute-done.25
  173.8 1.3 collective-permute-start.3
  175.2 1.3 collective-permute-start.4
  176.5 1.7 bitcast_dynamic-update-slice_fusion.11
  178.2 1.4 collective-permute-start.5
  179.9 6.5 collective-permute-start.7
  186.4 1.7 bitcast_dynamic-update-slice_fusion.10
  188.1 1.3 collective-permute-start.8
  189.6 31.6 %collective-permute-done.3 = bf16[512,2048]{1,0:T(8,128)(2,1)S(1)} collective-permute-done((bf16[512,2048]{1,0:T(8,128)(2,1)}, bf16[512,2048]{1,0:T(8,128)(2,1)S(1)}, u32[]{:S(2)}, u32[]{:S(2)}) %collective-permute-start.3) | collective-permute-done | bytes 2097184 | tf_op jit(solution)/shard_map/ppermute | solution.py:14
  221.2 1.3 collective-permute-start.9
  222.7 48.3 %collective-permute-done.4 = bf16[512,2048]{1,0:T(8,128)(2,1)S(1)} collective-permute-done((bf16[512,2048]{1,0:T(8,128)(2,1)}, bf16[512,2048]{1,0:T(8,128)(2,1)S(1)}, u32[]{:S(2)}, u32[]{:S(2)}) %collective-permute-start.4) | collective-permute-done | bytes 2097184 | tf_op jit(solution)/shard_map/ppermute | solution.py:14
  271.0 1.3 collective-permute-start.10
  272.5 108.9 %collective-permute-done.5 = bf16[512,2048]{1,0:T(8,128)(2,1)S(1)} collective-permute-done((bf16[512,2048]{1,0:T(8,128)(2,1)}, bf16[512,2048]{1,0:T(8,128)(2,1)S(1)}, u32[]{:S(2)}, u32[]{:S(2)}) %collective-permute-start.5) | collective-permute-done | bytes 2097184 | tf_op jit(solution)/shard_map/ppermute | solution.py:14
  381.4 1.5 collective-permute-start.11
  383.4 46.4 %collective-permute-done.8 = bf16[512,2048]{1,0:T(8,128)(2,1)S(1)} collective-permute-done((bf16[512,2048]{1,0:T(8,128)(2,1)S(1)}, bf16[512,2048]{1,0:T(8,128)(2,1)S(1)}, u32[]{:S(2)}, u32[]{:S(2)}) %collective-permute-start.8) | collective-permute-done | bytes 2097184 | tf_op jit(solution)/shard_map/ppermute | solution.py:14
  430.6 243.0 %collective-permute-done.11 = bf16[512,2048]{1,0:T(8,128)(2,1)S(1)} collective-permute-done((bf16[512,2048]{1,0:T(8,128)(2,1)S(1)}, bf16[512,2048]{1,0:T(8,128)(2,1)S(1)}, u32[]{:S(2)}, u32[]{:S(2)}) %collective-permute-start.11) | collective-permute-done | bytes 2097184 | tf_op jit(solution)/shard_map/ppermute | solution.py:14
  673.8 4.5 copy-done.2
  678.3 155.5 %while.10 = (s32[]{:T(128)}, bf16[4,128,2048]{2,1,0:T(8,128)(2,1)}, bf16[4,128,2048]{2,1,0:T(8,128)(2,1)}, s32[4,5]{1,0:T(4,128)S(1)}, bf16[24,128,2048]{2,1,0:T...) while((s32[]{:T(128)}, bf16[4,128,2048]{2,1,0:T(8,128)(2,1)}, ...), condition=%wide.region_3.5_spmd, body=%wide.region_0.4_spmd.sunk | while | flops 839126336 | bytes 81245688 | solution.py:113
  679.9 7.0 gather_fusion.2
  687.0 7.0 gather_fusion.1
  694.0 3.1 broadcast_select_fusion.6
  697.0 1.3 constant_dynamic-slice_fusion.11
  698.6 2.7 copy.49
  702.4 5.3 fusion.55
  707.7 2.1 fusion.56
  712.3 3.9 divide_convert_fusion.2
  718.8 7.0 gather_fusion.2
  725.8 7.0 gather_fusion.1
  732.8 3.1 broadcast_select_fusion.6
  735.9 1.3 constant_dynamic-slice_fusion.11
  737.5 2.7 copy.49
  741.3 5.3 fusion.55
  746.6 2.1 fusion.56
  751.1 3.9 divide_convert_fusion.2
  757.7 7.0 gather_fusion.2
  764.7 7.0 gather_fusion.1
  771.7 3.1 broadcast_select_fusion.6
  774.8 1.3 constant_dynamic-slice_fusion.11
  776.4 2.7 copy.49
  780.2 5.3 fusion.55
  785.5 2.1 fusion.56
  790.0 3.9 divide_convert_fusion.2
  796.6 7.0 gather_fusion.2
  803.6 7.0 gather_fusion.1
  810.6 3.1 broadcast_select_fusion.6
  813.7 1.3 constant_dynamic-slice_fusion.11
  815.2 2.7 copy.49
  819.1 5.3 fusion.55
  824.4 2.1 fusion.56
  828.9 3.9 divide_convert_fusion.2
  (184 shorter events, 39.0 us)
Async XLA Ops:
  0.0 8.9 %copy-start = (s32[64,5]{0,1:T(8,128)S(1)}, s32[64,5]{0,1:T(8,128)}, u32[]{:S(2)}) copy-start(s32[64,5]{0,1:T(8,128)} %param.15) | copy-start | bytes 3844
  0.0 10.4 %collective-permute-start.12 = (s32[2,512]{1,0:T(2,128)}, s32[2,512]{1,0:T(2,128)S(1)}, u32[]{:S(2)}, u32[]{:S(2)}) collective-permute-start(s32[2,512]{1,0:T(2,128)} %param.13), channel_id=1, source_target_pairs={{0,1},{1,2},{2,3},{3,4},{4,5},{5,6},{6,7},{7,8},{8,9},{9,10},{10,1... | collective-permute-start | bytes 12296 | tf_op jit(solution)/shard_map/ppermute | solution.py:75
  1.8 10.5 %collective-permute-start.13 = (s32[2,512]{1,0:T(2,128)}, s32[2,512]{1,0:T(2,128)S(1)}, u32[]{:S(2)}, u32[]{:S(2)}) collective-permute-start(s32[2,512]{1,0:T(2,128)} %param.13), channel_id=1, source_target_pairs={{0,15},{1,0},{2,1},{3,2},{4,3},{5,4},{6,5},{7,6},{8,7},{9,8},{10,9... | collective-permute-start | bytes 12296 | tf_op jit(solution)/shard_map/ppermute | solution.py:78
  1.8 173.3 %collective-permute-start = (bf16[512,2048]{1,0:T(8,128)(2,1)}, bf16[512,2048]{1,0:T(8,128)(2,1)}, u32[]{:S(2)}, u32[]{:S(2)}) collective-permute-start(bf16[512,2048]{1,0:T(8,128)(2,1)} %param.12), channel_id=1, source_target_pairs={{0,1},{1,2},{2,3},{3,4},{4,5},{5,6},{6,7},{7,8},{8,9},{9,10},{10,1... | collective-permute-start | bytes 6291464 | tf_op jit(solution)/shard_map/ppermute | solution.py:14
  5.5 174.4 %collective-permute-start.1 = (bf16[512,2048]{1,0:T(8,128)(2,1)}, bf16[512,2048]{1,0:T(8,128)(2,1)}, u32[]{:S(2)}, u32[]{:S(2)}) collective-permute-start(bf16[512,2048]{1,0:T(8,128)(2,1)} %param.12), channel_id=1, source_target_pairs={{0,2},{1,3},{2,4},{3,5},{4,6},{5,7},{6,8},{7,9},{8,10},{9,11},{10,... | collective-permute-start | bytes 6291464 | tf_op jit(solution)/shard_map/ppermute | solution.py:14
  7.4 180.7 %collective-permute-start.2 = (bf16[512,2048]{1,0:T(8,128)(2,1)}, bf16[512,2048]{1,0:T(8,128)(2,1)S(1)}, u32[]{:S(2)}, u32[]{:S(2)}) collective-permute-start(bf16[512,2048]{1,0:T(8,128)(2,1)} %param.12), channel_id=1, source_target_pairs={{0,3},{1,4},{2,5},{3,6},{4,7},{5,8},{6,9},{7,10},{8,11},{9,12},{10... | collective-permute-start | bytes 6291464 | tf_op jit(solution)/shard_map/ppermute | solution.py:14
  10.4 167.8 %collective-permute-start.6 = (bf16[512,2048]{1,0:T(8,128)(2,1)}, bf16[512,2048]{1,0:T(8,128)(2,1)S(1)}, u32[]{:S(2)}, u32[]{:S(2)}) collective-permute-start(bf16[512,2048]{1,0:T(8,128)(2,1)} %param.11), channel_id=1, source_target_pairs={{0,1},{1,2},{2,3},{3,4},{4,5},{5,6},{6,7},{7,8},{8,9},{9,10},{10,1... | collective-permute-start | bytes 6291464 | tf_op jit(solution)/shard_map/ppermute | solution.py:14
  12.3 106.3 %collective-permute-start.14 = (s32[2,512]{1,0:T(2,128)S(1)}, s32[2,512]{1,0:T(2,128)S(1)}, u32[]{:S(2)}, u32[]{:S(2)}) collective-permute-start(s32[2,512]{1,0:T(2,128)S(1)} %collective-permute-done.12), channel_id=1, source_target_pairs={{0,1},{1,2},{2,3},{3,4},{4,5},{5,6},{6,7},{7,8},{8,9},{9,10},{10,1... | collective-permute-start | bytes 12296 | tf_op jit(solution)/shard_map/ppermute | solution.py:75
  118.7 26.4 %collective-permute-start.15 = (s32[2,512]{1,0:T(2,128)S(1)}, s32[2,512]{1,0:T(2,128)S(1)}, u32[]{:S(2)}, u32[]{:S(2)}) collective-permute-start(s32[2,512]{1,0:T(2,128)S(1)} %collective-permute-done.13), channel_id=1, source_target_pairs={{0,15},{1,0},{2,1},{3,2},{4,3},{5,4},{6,5},{7,6},{8,7},{9,8},{10,9... | collective-permute-start | bytes 12296 | tf_op jit(solution)/shard_map/ppermute | solution.py:78
  145.0 1.2 collective-permute-start.16
  146.2 4.1 collective-permute-start.17
  150.3 1.2 collective-permute-start.18
  151.5 4.1 collective-permute-start.19
  155.6 1.2 collective-permute-start.20
  156.7 4.1 collective-permute-start.21
  160.8 1.2 collective-permute-start.22
  162.0 4.1 collective-permute-start.23
  166.1 1.2 collective-permute-start.24
  167.3 5.4 collective-permute-start.25
  172.7 1.2 collective-permute-start.26
  173.8 47.3 %collective-permute-start.3 = (bf16[512,2048]{1,0:T(8,128)(2,1)}, bf16[512,2048]{1,0:T(8,128)(2,1)S(1)}, u32[]{:S(2)}, u32[]{:S(2)}) collective-permute-start(bf16[512,2048]{1,0:T(8,128)(2,1)} %param.12), channel_id=1, source_target_pairs={{0,4},{1,5},{2,6},{3,7},{4,8},{5,9},{6,10},{7,11},{8,12},{9,13},{1... | collective-permute-start | bytes 6291464 | tf_op jit(solution)/shard_map/ppermute | solution.py:14
  175.2 95.8 %collective-permute-start.4 = (bf16[512,2048]{1,0:T(8,128)(2,1)}, bf16[512,2048]{1,0:T(8,128)(2,1)S(1)}, u32[]{:S(2)}, u32[]{:S(2)}) collective-permute-start(bf16[512,2048]{1,0:T(8,128)(2,1)} %param.12), channel_id=1, source_target_pairs={{0,5},{1,6},{2,7},{3,8},{4,9},{5,10},{6,11},{7,12},{8,13},{9,14},{... | collective-permute-start | bytes 6291464 | tf_op jit(solution)/shard_map/ppermute | solution.py:14
  178.2 1.7 copy-start.4
  178.2 203.2 %collective-permute-start.5 = (bf16[512,2048]{1,0:T(8,128)(2,1)}, bf16[512,2048]{1,0:T(8,128)(2,1)S(1)}, u32[]{:S(2)}, u32[]{:S(2)}) collective-permute-start(bf16[512,2048]{1,0:T(8,128)(2,1)} %param.12), channel_id=1, source_target_pairs={{0,6},{1,7},{2,8},{3,9},{4,10},{5,11},{6,12},{7,13},{8,14},{9,15},... | collective-permute-start | bytes 6291464 | tf_op jit(solution)/shard_map/ppermute | solution.py:14
  179.9 203.2 %collective-permute-start.7 = (bf16[512,2048]{1,0:T(8,128)(2,1)S(1)}, bf16[512,2048]{1,0:T(8,128)(2,1)S(1)}, u32[]{:S(2)}, u32[]{:S(2)}) collective-permute-start(bf16[512,2048]{1,0:T(8,128)(2,1)S(1)} %copy-done.4), channel_id=1, source_target_pairs={{0,2},{1,3},{2,4},{3,5},{4,6},{5,7},{6,8},{7,9},{8,10},{9,11},{10,... | collective-permute-start | bytes 6291464 | tf_op jit(solution)/shard_map/ppermute | solution.py:14
  188.1 241.7 %collective-permute-start.8 = (bf16[512,2048]{1,0:T(8,128)(2,1)S(1)}, bf16[512,2048]{1,0:T(8,128)(2,1)S(1)}, u32[]{:S(2)}, u32[]{:S(2)}) collective-permute-start(bf16[512,2048]{1,0:T(8,128)(2,1)S(1)} %copy-done.4), channel_id=1, source_target_pairs={{0,3},{1,4},{2,5},{3,6},{4,7},{5,8},{6,9},{7,10},{8,11},{9,12},{10... | collective-permute-start | bytes 6291464 | tf_op jit(solution)/shard_map/ppermute | solution.py:14
  221.2 208.9 %collective-permute-start.9 = (bf16[512,2048]{1,0:T(8,128)(2,1)S(1)}, bf16[512,2048]{1,0:T(8,128)(2,1)S(1)}, u32[]{:S(2)}, u32[]{:S(2)}) collective-permute-start(bf16[512,2048]{1,0:T(8,128)(2,1)S(1)} %copy-done.4), channel_id=1, source_target_pairs={{0,4},{1,5},{2,6},{3,7},{4,8},{5,9},{6,10},{7,11},{8,12},{9,13},{1... | collective-permute-start | bytes 6291464 | tf_op jit(solution)/shard_map/ppermute | solution.py:14
  271.0 159.4 %collective-permute-start.10 = (bf16[512,2048]{1,0:T(8,128)(2,1)S(1)}, bf16[512,2048]{1,0:T(8,128)(2,1)S(1)}, u32[]{:S(2)}, u32[]{:S(2)}) collective-permute-start(bf16[512,2048]{1,0:T(8,128)(2,1)S(1)} %copy-done.4), channel_id=1, source_target_pairs={{0,5},{1,6},{2,7},{3,8},{4,9},{5,10},{6,11},{7,12},{8,13},{9,14},{... | collective-permute-start | bytes 6291464 | tf_op jit(solution)/shard_map/ppermute | solution.py:14
  381.4 292.1 %collective-permute-start.11 = (bf16[512,2048]{1,0:T(8,128)(2,1)S(1)}, bf16[512,2048]{1,0:T(8,128)(2,1)S(1)}, u32[]{:S(2)}, u32[]{:S(2)}) collective-permute-start(bf16[512,2048]{1,0:T(8,128)(2,1)S(1)} %copy-done.4), channel_id=1, source_target_pairs={{0,6},{1,7},{2,8},{3,9},{4,10},{5,11},{6,12},{7,13},{8,14},{9,15},... | collective-permute-start | bytes 6291464 | tf_op jit(solution)/shard_map/ppermute | solution.py:14
  383.1 290.7 %copy-start.3 = (bf16[6,512,2048]{2,1,0:T(8,128)(2,1)}, bf16[6,512,2048]{2,1,0:T(8,128)(2,1)S(1)}, u32[]{:S(2)}) copy-start(bf16[6,512,2048]{2,1,0:T(8,128)(2,1)S(1)} %bitcast_dynamic-update-slice_fusion.6) | copy-start | bytes 37748740
  430.6 247.8 %copy-start.7 = (f32[16]{0:T(128)S(1)}, f32[16]{0:T(128)}, u32[]{:S(2)}) copy-start(f32[16]{0:T(128)} %param.14) | copy-start | bytes 196
  673.8 4.5 copy-start.2
  678.3 15.6 %copy-start.5 = (s32[64,2,128]{2,1,0:T(2,128)}, s32[64,2,128]{2,1,0:T(2,128)S(1)}, u32[]{:S(2)}) copy-start(s32[64,2,128]{2,1,0:T(2,128)S(1)} %get-tuple-element.282) | copy-start | bytes 196612 | tf_op jit(solution)/shard_map/while
  698.6 3.7 copy-start.8
  712.3 5.0 copy-start.6
  717.2 15.6 %copy-start.5 = (s32[64,2,128]{2,1,0:T(2,128)}, s32[64,2,128]{2,1,0:T(2,128)S(1)}, u32[]{:S(2)}) copy-start(s32[64,2,128]{2,1,0:T(2,128)S(1)} %get-tuple-element.282) | copy-start | bytes 196612 | tf_op jit(solution)/shard_map/while
  737.5 3.7 copy-start.8
  751.1 5.0 copy-start.6
  756.1 15.6 %copy-start.5 = (s32[64,2,128]{2,1,0:T(2,128)}, s32[64,2,128]{2,1,0:T(2,128)S(1)}, u32[]{:S(2)}) copy-start(s32[64,2,128]{2,1,0:T(2,128)S(1)} %get-tuple-element.282) | copy-start | bytes 196612 | tf_op jit(solution)/shard_map/while
  776.4 3.7 copy-start.8
  790.0 5.0 copy-start.6
  795.0 15.6 %copy-start.5 = (s32[64,2,128]{2,1,0:T(2,128)}, s32[64,2,128]{2,1,0:T(2,128)S(1)}, u32[]{:S(2)}) copy-start(s32[64,2,128]{2,1,0:T(2,128)S(1)} %get-tuple-element.282) | copy-start | bytes 196612 | tf_op jit(solution)/shard_map/while
  815.2 3.7 copy-start.8
  828.9 5.0 copy-start.6
  833.9 0.7 copy-start.1
